TPU v7x, 32 devices: a whole 2x2x4 slice. The times are simulated.
32 devices in a mesh: col: 4 (over y, x), dev: 4 (over z), ao: 2 (over core).
Axes of the slice: x: 2, y: 2, z: 4, core: 2. Of those that a mesh axis runs over, the one named last changes fastest.
Arguments:
- raw_ints: bfloat16 [1024, 32, 512], P('dev', None, 'col'), may hold values from -1.078125 to 1.078125
- metric: bfloat16 [1024, 1024], P('dev'), may hold values from -0.1875 to 0.1875
- amplitudes: bfloat16 [512, 512, 2048], P('col', 'dev', 'ao'), may hold values from -0.017944336 to 0.017944336
- pair_list: int32 [2, 2048], P(None, 'ao'), may hold values from 0 to 63
- occ_energy: float32 [64], replicated, may hold values from -2 to -0.3
- vir_energy: float32 [512], replicated, may hold values from 0.2 to 3
- window_ids: int32 [32], replicated, may hold values from 0 to 511, as said below
Outputs:
- residual: float32 [1024, 2048], P(('col', 'dev'), 'ao')
Inputs may be any that keep to these rules, and one draw needn't show every extreme that they name: `window_ids`: distinct virtual orbitals; 0 and 511 are always among them.
All inputs are finite; a program needn't handle non-finite values.
Results may differ from a plain program's by a relative error of at most 0.0041.
Values may be sent and summed in bfloat16 or wider, within the bound.
No kernel may reach another device: no remote copies, remote signals or barrier semaphores. Data moves between devices by JAX's collectives and lax.ppermute only.
A program may use at most 192 MiB of HBM per device.

v0:
```python
import jax
import jax.numpy as jnp
from jax import lax
from jax.sharding import PartitionSpec as P


def select_energy(positions, table):
    labels = jnp.arange(table.shape[0], dtype=jnp.int32)
    return jnp.sum(jnp.where(positions[:, None] == labels[None, :], table[None, :], 0.0), axis=1)


def on_device(raw_ints, metric, amplitudes, pair_list, occ_energy, vir_energy, window_ids):
    full_width = raw_ints.shape[1]
    portion = full_width // lax.axis_size("ao")
    own_rows = lax.dynamic_slice_in_dim(raw_ints, lax.axis_index("ao") * portion, portion, 1)
    local_aux = metric.shape[0]
    rows_used = own_rows.shape[1]
    c_block = own_rows.shape[2]
    raw_block = lax.all_gather(own_rows, "dev", axis=0, tiled=True)
    row_count = raw_block.shape[0]
    transformed = jnp.dot(
        metric,
        raw_block.reshape(row_count, rows_used * c_block),
        preferred_element_type=jnp.float32,
    )
    transformed = transformed.astype(jnp.bfloat16).reshape(local_aux, rows_used, c_block)
    spread = lax.all_gather(transformed, "col", axis=2, tiled=True)
    right_factor = lax.all_to_all(spread, "dev", split_axis=2, concat_axis=0, tiled=True)
    d_block = right_factor.shape[2]
    contract = (((0,), (0,)), ((), ()))
    left_factor = lax.all_gather(transformed, "dev", axis=0, tiled=True)
    right_factor = lax.all_gather(right_factor, "ao", axis=1, tiled=True)
    all_aux = left_factor.shape[0]
    own_ladder = lax.dot_general(
        left_factor.reshape(all_aux, rows_used * c_block),
        right_factor.reshape(all_aux, full_width * d_block),
        contract,
        preferred_element_type=jnp.float32,
    )
    ladder_flat = lax.all_gather(own_ladder.astype(jnp.bfloat16), "ao", axis=0, tiled=True)
    ladder = ladder_flat.reshape(full_width, c_block, full_width, d_block)
    ladder = jnp.transpose(ladder, (0, 2, 1, 3)).reshape(full_width * full_width, c_block * d_block)
    partial_value = jnp.dot(
        ladder,
        amplitudes.reshape(c_block * d_block, amplitudes.shape[2]),
        preferred_element_type=jnp.float32,
    )
    summed = lax.psum_scatter(partial_value, ("col", "dev"), scatter_dimension=0, tiled=True)
    row_total = summed.shape[0]
    global_rows = lax.axis_index(("col", "dev")) * row_total + jnp.arange(
        row_total, dtype=jnp.int32
    )
    window_energy = select_energy(window_ids, vir_energy)
    energy_first = select_energy(global_rows // full_width, window_energy)
    energy_second = select_energy(global_rows % full_width, window_energy)
    energy_i = select_energy(pair_list[0], occ_energy)
    energy_j = select_energy(pair_list[1], occ_energy)
    denominator = (energy_i + energy_j)[None, :] - (energy_first + energy_second)[:, None]
    return summed / denominator


def solution(mesh):
    in_specs = (
        P("dev", None, "col"),
        P("dev", None),
        P("col", "dev", "ao"),
        P(None, "ao"),
        P(),
        P(),
        P(),
    )
    out_specs = P(("col", "dev"), "ao")
    return jax.shard_map(
        on_device, mesh=mesh, in_specs=in_specs, out_specs=out_specs, check_vma=False
    )
```

profile of v0, /device:TPU:0, one launch (start us, length us, event | category | flops | bytes accessed | tf_op | source)
XLA Modules:
  0.0 614.5 jit_solution(7813897264550243271)
XLA Ops:
  6.5 1.6 copy-done
  8.1 1.1 constant_dynamic-slice_fusion
  9.3 0.0 all-gather.6.cloned.1.call-update
  9.3 0.0 all-gather.10.cloned.1.call-start
  9.3 83.6 %all-gather.6.cloned.1.call-done = bf16[1024,16,128]{2,1,0:T(8,128)(2,1)} async-done(((bf16[256,16,128]{2,1,0:T(8,128)(2,1)}), bf16[1024,16,128]{2,1,0:T(8,128)(2,1)}) %all-gather.6.cloned.1.call-update) | async-done | bytes 4194320 | tf_op jit(solution)/shard_map/all_gather | solution.py:19
  92.9 4.5 fusion.8
  97.4 1.6 copy.19
  98.9 0.0 all-gather.10.cloned.1.call-update
  99.0 51.2 %all-gather.10.cloned.1.call-done = bf16[256,16,512]{0,1,2:T(8,128)(2,1)} async-done(((bf16[256,16,128]{0,1,2:T(8,128)(2,1)}), bf16[256,16,512]{0,1,2:T(8,128)(2,1)}) %all-gather.10.cloned.1.call-update) | async-done | bytes 4194320 | tf_op jit(solution)/shard_map/all_gather | solution.py:27
  150.2 4.8 all-to-all-start
  155.0 0.0 all-gather.8.cloned.1.call-start
  155.1 0.7 all-gather.8.cloned.1.call-update
  155.8 0.0 all-gather.12.cloned.1.call-start
  155.8 159.9 %all-to-all-done = bf16[256,16,512]{0,1,2:T(8,128)(2,1)} async-done(((bf16[256,16,512]{0,1,2:T(8,128)(2,1)}), bf16[256,16,512]{0,1,2:T(8,128)(2,1)}, u32[]{:S(2)}, u32[]{:S(2)}) %all-to-all-start) | async-done | bytes 4194336 | tf_op jit(solution)/shard_map/all_to_all | solution.py:28
  315.8 9.0 %copy.21 = bf16[4,256,16,128]{3,2,1,0:T(8,128)(2,1)} copy(bf16[4,256,16,128]{1,2,3,0:T(8,128)(2,1)} %bitcast.6) | data formatting | bytes 8388608 | tf_op jit(solution)/shard_map/all_to_all | solution.py:28
  324.7 0.0 all-gather.12.cloned.1.call-update
  324.7 0.0 all-gather.14.cloned.1.call-start
  324.8 0.0 all-gather.8.cloned.1.call-done
  324.8 16.3 %all-gather.12.cloned.1.call-done = bf16[1024,32,128]{2,1,0:T(8,128)(2,1)} async-done(((bf16[1024,16,128]{2,1,0:T(8,128)(2,1)}), bf16[1024,32,128]{2,1,0:T(8,128)(2,1)}) %all-gather.12.cloned.1.call-update) | async-done | bytes 8388624 | tf_op jit(solution)/shard_map/all_gather | solution.py:32
  341.1 24.3 %convolution_convert_fusion = bf16[2048,4096]{1,0:T(8,128)(2,1)} fusion(bf16[1024,2048]{0,1:T(8,128)(2,1)} %bitcast.43, bf16[128,8,32,128]{3,2,1,0:T(8,128)(2,1)} %bitcast.42), kind=kOutput, calls=%fused_computation.3 | convolution fusion | flops 17188257792 | bytes 29360128 | tf_op jit(solution)/shard_map/dot_general | solution.py:34
  365.5 0.0 all-gather.14.cloned.1.call-update
  365.5 0.2 reduce-scatter.2.cloned.1.call-start
  365.7 52.1 %all-gather.14.cloned.1.call-done = bf16[4096,4096]{1,0:T(8,128)(2,1)} async-done(((bf16[2048,4096]{1,0:T(8,128)(2,1)}), bf16[4096,4096]{1,0:T(8,128)(2,1)}) %all-gather.14.cloned.1.call-update) | async-done | bytes 33554448 | tf_op jit(solution)/shard_map/all_gather | solution.py:40
  417.9 23.1 %copy.26 = bf16[512,8,32,128]{3,2,1,0:T(8,128)(2,1)} copy(bf16[512,8,32,128]{3,1,2,0:T(8,128)(2,1)} %bitcast.34) | data formatting | bytes 67108864
  440.9 23.0 %copy.22 = bf16[32,128,32,128]{3,1,2,0:T(8,128)(2,1)} copy(bf16[32,128,32,128]{3,2,1,0:T(8,128)(2,1)} %bitcast.33) | data formatting | bytes 67108864 | tf_op jit(solution)/shard_map/reshape | solution.py:41
  464.0 43.1 %fusion = f32[1024,1024]{1,0:T(8,128)} fusion(bf16[16384,1024]{1,0:T(8,128)(2,1)} %bitcast.41, bf16[128,8,128,128]{3,2,1,0:T(8,128)(2,1)} %bitcast.35), kind=kOutput, calls=%fused_computation | convolution fusion | flops 34359738368 | bytes 71303168 | tf_op jit(solution)/shard_map/dot_general | solution.py:43
  507.1 0.0 reduce-scatter.2.cloned.1.call-update
  507.2 0.2 select_reduce_fusion.2
  507.4 0.1 select_reduce_fusion.3
  507.5 0.2 select_reduce_fusion
  507.7 98.2 %reduce-scatter.2.cloned.1.call-done = f32[64,1024]{1,0:T(8,128)} async-done(((f32[1024,1024]{1,0:T(8,128)}), f32[64,1024]{1,0:T(8,128)}) %reduce-scatter.2.cloned.1.call-update) | async-done | bytes 262160 | tf_op jit(solution)/shard_map/reduce_scatter | solution.py:48
  605.8 1.8 subtract_divide_fusion
  (18 shorter events, 0.1 us)
Async XLA Ops:
  6.5 1.6 copy-start
  6.5 86.4 %all-gather.6.cloned.1.call-start = ((), (), s32[]{:S(2)}) async-start(), calls=%async_computation.2 | async-start | bytes 5242880 | tf_op jit(solution)/shard_map/all_gather | solution.py:19
  9.3 140.9 %all-gather.10.cloned.1.call-start = ((), (), s32[]{:S(2)}) async-start(), calls=%async_computation.4 | async-start | bytes 5242880 | tf_op jit(solution)/shard_map/all_gather | solution.py:27
  97.4 57.7 %copy-start.2 = (bf16[2048,256]{1,0:T(8,128)(2,1)}, bf16[2048,256]{1,0:T(8,128)(2,1)S(1)}, u32[]{:S(2)}) copy-start(bf16[2048,256]{1,0:T(8,128)(2,1)S(1)} %fusion.8) | copy-start | bytes 3145732
  150.2 165.6 %all-to-all-start = ((bf16[256,16,512]{0,1,2:T(8,128)(2,1)}), bf16[256,16,512]{0,1,2:T(8,128)(2,1)}, u32[]{:S(2)}, u32[]{:S(2)}) async-start(bf16[256,16,512]{0,1,2:T(8,128)(2,1)} %all-gather.10.cloned.1.call-done), calls=%async_computation | async-start | bytes 8388608 | tf_op jit(solution)/shard_map/all_to_all | solution.py:28
  155.0 169.8 %all-gather.8.cloned.1.call-start = ((), (), s32[]{:S(2)}) async-start(), calls=%async_computation.3 | async-start | bytes 5242880 | tf_op jit(solution)/shard_map/all_gather | solution.py:31
  155.8 185.3 %all-gather.12.cloned.1.call-start = ((), (), s32[]{:S(2)}) async-start(), calls=%async_computation.5 | async-start | bytes 12582912 | tf_op jit(solution)/shard_map/all_gather | solution.py:32
  324.7 93.1 %all-gather.14.cloned.1.call-start = ((), (), s32[]{:S(2)}) async-start(), calls=%async_computation.6 | async-start | bytes 50331648 | tf_op jit(solution)/shard_map/all_gather | solution.py:40
  365.5 240.4 %reduce-scatter.2.cloned.1.call-start = ((), (), s32[]{:S(2)}) async-start(), calls=%async_computation.7 | async-start | bytes 4456448 | tf_op jit(solution)/shard_map/reduce_scatter | solution.py:48
  464.0 43.2 %copy-start.4 = (f32[512]{0:T(512)S(1)}, f32[512]{0:T(512)}, u32[]{:S(2)}) copy-start(f32[512]{0:T(512)} %param.12) | copy-start | bytes 6148
  464.0 43.2 %copy-start.6 = (s32[32]{0:T(128)S(1)}, s32[32]{0:T(128)}, u32[]{:S(2)}) copy-start(s32[32]{0:T(128)} %param.13) | copy-start | bytes 388
  464.0 43.5 %copy-start.3 = (s32[2,1024]{1,0:T(2,128)S(1)}, s32[2,1024]{1,0:T(2,128)}, u32[]{:S(2)}) copy-start(s32[2,1024]{1,0:T(2,128)} %param.10) | copy-start | bytes 24580
  464.0 43.5 %copy-start.5 = (f32[64]{0:T(128)S(1)}, f32[64]{0:T(128)}, u32[]{:S(2)}) copy-start(f32[64]{0:T(128)} %param.11) | copy-start | bytes 772
  464.0 143.6 %copy-start.1 = (bf16[256,32,128]{2,1,0:T(8,128)(2,1)S(1)}, bf16[256,32,128]{2,1,0:T(8,128)(2,1)}, u32[]{:S(2)}) copy-start(bf16[256,32,128]{2,1,0:T(8,128)(2,1)} %param.7) | copy-start | bytes 6291460
Sparse Core Ops, SparseCore 0:
  9.4 83.4 all-gather.5
  99.1 51.0 all-gather.9
  157.4 150.1 all-gather.7
  324.9 16.1 all-gather.11
  365.6 52.2 all-gather.13
  507.2 98.5 reduce-scatter.1
where the time goes:
time: 615 us; the launch traced here: 614 us
  waiting for transfers between devices  462 us (75%)
  matrix products  71.9 us (12%)
  local copies, waits for them, and re-layouts  59.4 us (10%)
  between operations  13.6 us (2%)
    all_to_all x1, waiting for transfers between devices, on_device(): lax.all_to_all(spread, 'dev', split_axis=2, concat_axis=0, tiled=True)  160 us
    reduce_scatter x1, waiting for transfers between devices, on_device(): lax.psum_scatter(partial_value, ('col', 'dev'), scatter_dimension=0, tile...  98.2 us
    all_gather x1, waiting for transfers between devices, on_device(): raw_block = lax.all_gather(own_rows, 'dev', axis=0, tiled=True)  83.6 us
    all_gather x1, waiting for transfers between devices, on_device(): lax.all_gather(own_ladder.astype(jnp.bfloat16), 'ao', axis=0, tiled=True)  52.1 us
    all_gather x1, waiting for transfers between devices, on_device(): spread = lax.all_gather(transformed, 'col', axis=2, tiled=True)  51.2 us
    dot_general x1, matrix products, on_device(): jnp.dot(ladder, amplitudes.reshape(c_block * d_block, amplitudes.shape[2]...  43.1 us
    unnamed x15, local copies, waits for them, and re-layouts  24.7 us
    dot_general x1, matrix products, on_device(): lax.dot_general(left_factor.reshape(all_aux, rows_used * c_block), right_...  24.3 us
  transfers between devices with their start and end apart: 7, of which 6 were waited for; matrix products, arithmetic and copies ran while one was open for 2% of the time, Pallas kernels for 0%

commit v1 on v0

--- a/solution.py
+++ b/solution.py
@@ -2,6 +2,27 @@
 import jax.numpy as jnp
 from jax import lax
 from jax.sharding import PartitionSpec as P
+
+
+def collect(x, axis, dim):
+    size, index, width = (lax.axis_size(axis), lax.axis_index(axis), x.shape[dim])
+    ahead = [(i, (i + 1) % size) for i in range(size)]
+    downward = [(i, (i - 1) % size) for i in range(size)]
+    out = jnp.zeros((*x.shape[:dim], size * width, *x.shape[dim + 1 :]), x.dtype)
+    out = lax.dynamic_update_slice_in_dim(out, x, index * width, axis=dim)
+    from_left = from_right = x
+    halfway = size // 2
+    for step in range(1, halfway + 1):
+        from_left = lax.ppermute(from_left, axis, ahead)
+        out = lax.dynamic_update_slice_in_dim(
+            out, from_left, (index - step) % size * width, axis=dim
+        )
+        if step < size - halfway:
+            from_right = lax.ppermute(from_right, axis, downward)
+            out = lax.dynamic_update_slice_in_dim(
+                out, from_right, (index + step) % size * width, axis=dim
+            )
+    return out
 
 
 def select_energy(positions, table):
@@ -24,7 +45,7 @@
         preferred_element_type=jnp.float32,
     )
     transformed = transformed.astype(jnp.bfloat16).reshape(local_aux, rows_used, c_block)
-    spread = lax.all_gather(transformed, "col", axis=2, tiled=True)
+    spread = collect(transformed, "col", 2)
     right_factor = lax.all_to_all(spread, "dev", split_axis=2, concat_axis=0, tiled=True)
     d_block = right_factor.shape[2]
     contract = (((0,), (0,)), ((), ()))

time: 615 us -> 637 us (1.036)
  waiting for transfers between devices: 462 us -> 473 us
  local copies, waits for them, and re-layouts: 59.4 us -> 67.1 us
    ppermute x0 -> x3, waiting for transfers between devices: none -> 63.9 us  [the longest x2 42.9 us: collect(): from_left = lax.ppermute(from_left, axis, ahead)]
    all_gather x1 -> x0, waiting for transfers between devices: 51.2 us -> none  [on_device(): spread = lax.all_gather(transformed, 'col', axis=2, tiled=True)]
  transfers between devices with their start and end apart: 7 -> 9, of which waited for: 6 -> 8; matrix products, arithmetic and copies ran while one was open for 2% -> 2% of each run, Pallas kernels for 0% -> 0%
where the time goes in v1:
time: 637 us
  waiting for transfers between devices  473 us (74%)
  matrix products  71.9 us (11%)
  local copies, waits for them, and re-layouts  67.1 us (11%)
  between operations  13.3 us (2%)
  starting transfers between devices  8.77 us (1%)
    all_to_all x1, waiting for transfers between devices, on_device(): lax.all_to_all(spread, 'dev', split_axis=2, concat_axis=0, tiled=True)  159 us
    reduce_scatter x1, waiting for transfers between devices, on_device(): lax.psum_scatter(partial_value, ('col', 'dev'), scatter_dimension=0, tile...  97.6 us
    all_gather x1, waiting for transfers between devices, on_device(): raw_block = lax.all_gather(own_rows, 'dev', axis=0, tiled=True)  83.6 us
    all_gather x1, waiting for transfers between devices, on_device(): lax.all_gather(own_ladder.astype(jnp.bfloat16), 'ao', axis=0, tiled=True)  52.2 us
    dot_general x1, matrix products, on_device(): jnp.dot(ladder, amplitudes.reshape(c_block * d_block, amplitudes.shape[2]...  43.1 us
    ppermute x2, waiting for transfers between devices, collect(): from_left = lax.ppermute(from_left, axis, ahead)  42.9 us
    unnamed x15, local copies, waits for them, and re-layouts  25.3 us
    dot_general x1, matrix products, on_device(): lax.dot_general(left_factor.reshape(all_aux, rows_used * c_block), right_...  24.3 us
  transfers between devices with their start and end apart: 9, of which 8 were waited for; matrix products, arithmetic and copies ran while one was open for 2% of the time, Pallas kernels for 0%

profile of v1, /device:TPU:0, one launch (start us, length us, event | category | flops | bytes accessed | tf_op | source)
XLA Modules:
  0.0 636.7 jit_solution(5414142721861886599)
XLA Ops:
  6.5 1.6 copy-done
  8.1 1.2 constant_dynamic-slice_fusion
  9.3 83.6 %all-gather.5.cloned.1.call-done = bf16[1024,16,128]{2,1,0:T(8,128)(2,1)} async-done(((bf16[256,16,128]{2,1,0:T(8,128)(2,1)}), bf16[1024,16,128]{2,1,0:T(8,128)(2,1)}) %all-gather.5.cloned.1.call-update) | async-done | bytes 4194320 | tf_op jit(solution)/shard_map/all_gather | solution.py:40
  92.9 4.5 fusion.8
  97.4 2.3 broadcast_in_dim.62
  99.7 1.9 fusion.11
  101.6 1.5 collective-permute-start
  103.2 1.4 collective-permute-start.1
  104.5 24.2 %collective-permute-done = bf16[256,16,128]{0,1,2:T(8,128)(2,1)S(1)} collective-permute-done((bf16[256,16,128]{0,1,2:T(8,128)(2,1)}, bf16[256,16,128]{0,1,2:T(8,128)(2,1)S(1)}, u32[]{:S(2)}, u32[]{:S(2)}) %collective-permute-start) | collective-permute-done | bytes 1048608 | tf_op jit(solution)/shard_map/ppermute | solution.py:16
  128.8 0.6 collective-permute-start.2
  129.4 1.1 constant_dynamic-update-slice_fusion.2
  130.5 20.9 %collective-permute-done.1 = bf16[256,16,128]{0,1,2:T(8,128)(2,1)} collective-permute-done((bf16[256,16,128]{0,1,2:T(8,128)(2,1)}, bf16[256,16,128]{0,1,2:T(8,128)(2,1)}, u32[]{:S(2)}, u32[]{:S(2)}) %collective-permute-start.1) | collective-permute-done | bytes 1048608 | tf_op jit(solution)/shard_map/ppermute | solution.py:21
  151.4 2.3 constant_dynamic-update-slice_fusion.1
  153.7 18.7 %collective-permute-done.2 = bf16[256,16,128]{0,1,2:T(8,128)(2,1)S(1)} collective-permute-done((bf16[256,16,128]{0,1,2:T(8,128)(2,1)S(1)}, bf16[256,16,128]{0,1,2:T(8,128)(2,1)S(1)}, u32[]{:S(2)}, u32[]{:S(2)}) %collective-permute-start.2) | collective-permute-done | bytes 1048608 | tf_op jit(solution)/shard_map/ppermute | solution.py:16
  172.4 1.1 constant_dynamic-update-slice_fusion
  173.5 4.8 all-to-all-start
  178.4 0.7 all-gather.7.cloned.1.call-update
  179.2 159.1 %all-to-all-done = bf16[256,16,512]{0,1,2:T(8,128)(2,1)} async-done(((bf16[256,16,512]{0,1,2:T(8,128)(2,1)}), bf16[256,16,512]{0,1,2:T(8,128)(2,1)}, u32[]{:S(2)}, u32[]{:S(2)}) %all-to-all-start) | async-done | bytes 4194336 | tf_op jit(solution)/shard_map/all_to_all | solution.py:49
  338.3 9.0 %copy.21 = bf16[4,256,16,128]{3,2,1,0:T(8,128)(2,1)} copy(bf16[4,256,16,128]{1,2,3,0:T(8,128)(2,1)} %bitcast.6) | data formatting | bytes 8388608 | tf_op jit(solution)/shard_map/all_to_all | solution.py:49
  347.3 16.3 %all-gather.9.cloned.1.call-done = bf16[1024,32,128]{2,1,0:T(8,128)(2,1)} async-done(((bf16[1024,16,128]{2,1,0:T(8,128)(2,1)}), bf16[1024,32,128]{2,1,0:T(8,128)(2,1)}) %all-gather.9.cloned.1.call-update) | async-done | bytes 8388624 | tf_op jit(solution)/shard_map/all_gather | solution.py:53
  363.6 24.3 %convolution_convert_fusion = bf16[2048,4096]{1,0:T(8,128)(2,1)} fusion(bf16[1024,2048]{0,1:T(8,128)(2,1)} %bitcast.43, bf16[128,8,32,128]{3,2,1,0:T(8,128)(2,1)} %bitcast.42), kind=kOutput, calls=%fused_computation.3 | convolution fusion | flops 17188257792 | bytes 29360128 | tf_op jit(solution)/shard_map/dot_general | solution.py:55
  388.0 0.2 reduce-scatter.2.cloned.1.call-start
  388.2 52.2 %all-gather.11.cloned.1.call-done = bf16[4096,4096]{1,0:T(8,128)(2,1)} async-done(((bf16[2048,4096]{1,0:T(8,128)(2,1)}), bf16[4096,4096]{1,0:T(8,128)(2,1)}) %all-gather.11.cloned.1.call-update) | async-done | bytes 33554448 | tf_op jit(solution)/shard_map/all_gather | solution.py:61
  440.4 23.1 %copy.26 = bf16[512,8,32,128]{3,2,1,0:T(8,128)(2,1)} copy(bf16[512,8,32,128]{3,1,2,0:T(8,128)(2,1)} %bitcast.34) | data formatting | bytes 67108864
  463.4 23.1 %copy.22 = bf16[32,128,32,128]{3,1,2,0:T(8,128)(2,1)} copy(bf16[32,128,32,128]{3,2,1,0:T(8,128)(2,1)} %bitcast.33) | data formatting | bytes 67108864 | tf_op jit(solution)/shard_map/reshape | solution.py:62
  486.5 43.1 %fusion = f32[1024,1024]{1,0:T(8,128)} fusion(bf16[16384,1024]{1,0:T(8,128)(2,1)} %bitcast.41, bf16[128,8,128,128]{3,2,1,0:T(8,128)(2,1)} %bitcast.35), kind=kOutput, calls=%fused_computation | convolution fusion | flops 34359738368 | bytes 71303168 | tf_op jit(solution)/shard_map/dot_general | solution.py:64
  529.7 0.6 copy-done.4
  530.3 0.2 select_reduce_fusion.2
  530.4 0.1 select_reduce_fusion.3
  530.6 0.2 select_reduce_fusion
  530.8 97.6 %reduce-scatter.2.cloned.1.call-done = f32[64,1024]{1,0:T(8,128)} async-done(((f32[1024,1024]{1,0:T(8,128)}), f32[64,1024]{1,0:T(8,128)}) %reduce-scatter.2.cloned.1.call-update) | async-done | bytes 262160 | tf_op jit(solution)/shard_map/reduce_scatter | solution.py:69
  628.4 1.8 subtract_divide_fusion
  (25 shorter events, 0.3 us)
Async XLA Ops:
  6.5 1.6 copy-start
  6.5 86.4 %all-gather.5.cloned.1.call-start = ((), (), s32[]{:S(2)}) async-start(), calls=%async_computation.2 | async-start | bytes 5242880 | tf_op jit(solution)/shard_map/all_gather | solution.py:40
  97.4 33.1 %copy-start.2 = (bf16[2048,256]{1,0:T(8,128)(2,1)}, bf16[2048,256]{1,0:T(8,128)(2,1)S(1)}, u32[]{:S(2)}) copy-start(bf16[2048,256]{1,0:T(8,128)(2,1)S(1)} %fusion.8) | copy-start | bytes 3145732
  101.6 27.1 %collective-permute-start = (bf16[256,16,128]{0,1,2:T(8,128)(2,1)}, bf16[256,16,128]{0,1,2:T(8,128)(2,1)S(1)}, u32[]{:S(2)}, u32[]{:S(2)}) collective-permute-start(bf16[256,16,128]{0,1,2:T(8,128)(2,1)} %get-tuple-element.9), channel_id=1, source_target_pairs={{0,8},{8,16},{16,24},{24,0},{1,9},{9,17},{17,25},{25,1},{2,10},{10... | collective-permute-start | bytes 3145736 | tf_op jit(solution)/shard_map/ppermute | solution.py:16
  103.2 48.2 %collective-permute-start.1 = (bf16[256,16,128]{0,1,2:T(8,128)(2,1)}, bf16[256,16,128]{0,1,2:T(8,128)(2,1)}, u32[]{:S(2)}, u32[]{:S(2)}) collective-permute-start(bf16[256,16,128]{0,1,2:T(8,128)(2,1)} %get-tuple-element.9), channel_id=1, source_target_pairs={{0,24},{8,0},{16,8},{24,16},{1,25},{9,1},{17,9},{25,17},{2,26},{10... | collective-permute-start | bytes 3145736 | tf_op jit(solution)/shard_map/ppermute | solution.py:21
  128.8 43.7 %collective-permute-start.2 = (bf16[256,16,128]{0,1,2:T(8,128)(2,1)S(1)}, bf16[256,16,128]{0,1,2:T(8,128)(2,1)S(1)}, u32[]{:S(2)}, u32[]{:S(2)}) collective-permute-start(bf16[256,16,128]{0,1,2:T(8,128)(2,1)S(1)} %collective-permute-done), channel_id=1, source_target_pairs={{0,8},{8,16},{16,24},{24,0},{1,9},{9,17},{17,25},{25,1},{2,10},{10... | collective-permute-start | bytes 3145736 | tf_op jit(solution)/shard_map/ppermute | solution.py:16
  173.5 164.8 %all-to-all-start = ((bf16[256,16,512]{0,1,2:T(8,128)(2,1)}), bf16[256,16,512]{0,1,2:T(8,128)(2,1)}, u32[]{:S(2)}, u32[]{:S(2)}) async-start(bf16[256,16,512]{0,1,2:T(8,128)(2,1)} %constant_dynamic-update-slice_fusion), calls=%async_computation | async-start | bytes 8388608 | tf_op jit(solution)/shard_map/all_to_all | solution.py:49
  178.4 168.9 %all-gather.7.cloned.1.call-start = ((), (), s32[]{:S(2)}) async-start(), calls=%async_computation.3 | async-start | bytes 5242880 | tf_op jit(solution)/shard_map/all_gather | solution.py:52
  179.1 184.5 %all-gather.9.cloned.1.call-start = ((), (), s32[]{:S(2)}) async-start(), calls=%async_computation.4 | async-start | bytes 12582912 | tf_op jit(solution)/shard_map/all_gather | solution.py:53
  347.2 93.1 %all-gather.11.cloned.1.call-start = ((), (), s32[]{:S(2)}) async-start(), calls=%async_computation.5 | async-start | bytes 50331648 | tf_op jit(solution)/shard_map/all_gather | solution.py:61
  388.0 240.4 %reduce-scatter.2.cloned.1.call-start = ((), (), s32[]{:S(2)}) async-start(), calls=%async_computation.6 | async-start | bytes 4456448 | tf_op jit(solution)/shard_map/reduce_scatter | solution.py:69
  486.5 143.7 %copy-start.1 = (bf16[256,32,128]{2,1,0:T(8,128)(2,1)S(1)}, bf16[256,32,128]{2,1,0:T(8,128)(2,1)}, u32[]{:S(2)}) copy-start(bf16[256,32,128]{2,1,0:T(8,128)(2,1)} %param.7) | copy-start | bytes 6291460
  529.6 0.7 copy-start.4
  529.6 0.7 copy-start.6
  529.6 1.0 copy-start.3
  529.6 1.0 copy-start.5
Sparse Core Ops, SparseCore 0:
  9.4 83.4 all-gather.4
  180.7 150.5 all-gather.6
  347.4 16.2 all-gather.8
  388.1 52.2 all-gather.10
  529.7 98.6 reduce-scatter.1
